TPU v7x, 32 devices: a whole 2x2x4 slice. The times are simulated.
32 devices in a mesh: grp: 2 (over x), tile: 16 (over z, y, core).
Axes of the slice: x: 2, y: 2, z: 4, core: 2. Of those that a mesh axis runs over, the one named last changes fastest.
Arguments:
- visibility: bfloat16 [32, 16, 2, 256, 256], P('tile', 'grp'), parts along dimension 1, may hold values from -12 to 12
- station_beam: bfloat16 [16, 2, 512, 2048], P('grp', None, 'tile'), parts along dimension 0, may hold values from -4.1875 to 4.1875
- antenna_uvw: float32 [16, 3, 2048], P('grp'), parts along dimension 0, may hold values from -40 to 40
- source_dirs: float32 [2, 4096], P(None, 'tile'), may hold values from -0.4 to 0.4
- source_flux: bfloat16 [8192], P(('grp', 'tile')), parts along dimension 0, may hold values from 0.0029907227 to 0.029907227
- visible_list: int32 [8, 512], P(None, 'tile'), may hold values from 0 to 255
- antenna_flags: int32 [16, 2048], P('grp'), parts along dimension 0, may hold values 0 or 1
Outputs:
- residual: bfloat16 [32, 16, 2, 256, 256], P('tile', 'grp'), parts along dimension 1
- flux_grad: float32 [16, 512], P('grp', 'tile'), parts along dimension 0
There are 2 independent parts, one for each index of `grp`. A program takes and returns all parts, laid end to end along the dimension named above; an argument that names none is the same for every part. Nothing has to cross between parts.
Inputs may be any that keep to these rules, and one draw needn't show every extreme that they name: `visible_list`: entry k of a slot names pool source 256 * (k // 32) + value, a source of its own group. `antenna_flags`: 1 marks a flagged antenna.
All inputs are finite; a program needn't handle non-finite values.
Results may differ from a plain program's by a relative error of at most 0.0034.
Values may be sent and summed in bfloat16 or wider, within the bound.
A program may use at most 192 MiB of HBM per device.

v0:
```python
import math

import jax
import jax.numpy as jnp
import numpy as np
from jax import lax
from jax.sharding import PartitionSpec as P

BLOCKS = 8


two_pi = 2.0 * math.pi


def unit_table(block_count):
    first_list = []
    second_list = []
    diag_list = []
    for row_block in range(block_count):
        for col_block in range(row_block + 1, block_count):
            first_list.append(row_block)
            second_list.append(col_block)
            diag_list.append(0)
    for pair_index in range(block_count // 2):
        first_list.append(2 * pair_index)
        second_list.append(2 * pair_index + 1)
        diag_list.append(1)
    return (
        np.array(first_list, np.int32),
        np.array(second_list, np.int32),
        np.array(diag_list, np.int32),
    )


def build_factors(station_beam, antenna_uvw, source_dirs, source_flux, visible_list):
    pool_size = source_dirs.shape[1]
    chosen = visible_list[:, :, None] == jnp.arange(pool_size, dtype=jnp.int32)[None, None, :]
    coord_east = jnp.sum(jnp.where(chosen, source_dirs[0][None, None, :], 0.0), axis=2)
    coord_north = jnp.sum(jnp.where(chosen, source_dirs[1][None, None, :], 0.0), axis=2)
    brightness = jnp.sum(
        jnp.where(chosen, source_flux.astype(jnp.float32)[None, None, :], 0.0), axis=2
    ).astype(jnp.bfloat16)
    depth_term = jnp.sqrt(1.0 - coord_east * coord_east - coord_north * coord_north) - 1.0
    delay_sum = (
        antenna_uvw[:, 0, None, :] * coord_east[:, :, None]
        + antenna_uvw[:, 1, None, :] * coord_north[:, :, None]
        + antenna_uvw[:, 2, None, :] * depth_term[:, :, None]
    )
    phases = two_pi * delay_sum
    cosine = jnp.cos(phases)
    sine = jnp.sin(phases)
    beam_f = station_beam.astype(jnp.float32)
    real_part = beam_f[:, 0] * cosine + beam_f[:, 1] * sine
    imag_part = beam_f[:, 1] * cosine - beam_f[:, 0] * sine
    return (jnp.stack([real_part, imag_part], 1).astype(jnp.bfloat16), brightness)


def predict(rows_f, cols_f, brightness):
    scaled = (rows_f.astype(jnp.float32) * brightness.astype(jnp.float32)[:, None, :, None]).astype(
        jnp.bfloat16
    )
    turned = jnp.stack([scaled[:, 1], -scaled[:, 0]], 1)
    stacked = jnp.stack([scaled, turned], 1)
    return jnp.einsum("tdckr,tckq->tdrq", stacked, cols_f, preferred_element_type=jnp.float32)


def pull_back(resid, rows_f, cols_f):
    rstack = jnp.stack(
        [jnp.stack([resid[:, 0], -resid[:, 1]], 1), jnp.stack([resid[:, 1], resid[:, 0]], 1)], 1
    )
    pulled = jnp.einsum("tdcrq,tckq->tdkr", rstack, cols_f, preferred_element_type=jnp.float32)
    return jnp.sum(rows_f.astype(jnp.float32) * pulled, axis=(1, 3))


def unit_work(block_one, block_two, diag_tile, bright_all, vis_unit, keep_one, keep_two):
    span = vis_unit.shape[3]
    local_ids = jnp.arange(span, dtype=jnp.int32)
    upper_part = local_ids[:, None] < local_ids[None, :]
    lower_part = local_ids[:, None] > local_ids[None, :]
    cols_one = jnp.where(diag_tile, block_one, block_two)
    first_pred = predict(block_one, cols_one, bright_all)
    pred_shape = first_pred.shape
    second_pred = lax.cond(
        diag_tile,
        lambda: predict(block_two, block_two, bright_all),
        lambda: jnp.zeros(pred_shape, jnp.float32),
    )
    first_mask = jnp.logical_or(jnp.logical_not(diag_tile), upper_part)
    predicted = jnp.where(first_mask[None, None], first_pred, jnp.swapaxes(second_pred, 2, 3))
    upper_f = upper_part.astype(jnp.float32)
    lower_f = lower_part.astype(jnp.float32)
    off_weight = keep_one[:, :, None] * keep_two[:, None, :]
    diag_weight = (
        upper_f[None] * keep_one[:, :, None] * keep_one[:, None, :]
        + lower_f[None] * keep_two[:, :, None] * keep_two[:, None, :]
    )
    weights = jnp.where(diag_tile, diag_weight, off_weight)
    residual = (weights[:, None] * (vis_unit.astype(jnp.float32) - predicted)).astype(jnp.bfloat16)
    zero_res = jnp.zeros_like(residual)
    first_res = jnp.where(first_mask[None, None], residual, zero_res)
    partial_value = pull_back(first_res, block_one, cols_one)
    second_sel = jnp.logical_and(diag_tile, lower_part)
    grad_shape = partial_value.shape
    second_part = lax.cond(
        diag_tile,
        lambda: pull_back(
            jnp.swapaxes(jnp.where(second_sel[None, None], residual, zero_res), 2, 3),
            block_two,
            block_two,
        ),
        lambda: jnp.zeros(grad_shape, jnp.float32),
    )
    return (residual, partial_value + second_part)


def per_device(
    visibility, station_beam, antenna_uvw, source_dirs, source_flux, visible_list, antenna_flags
):
    tile_count = lax.axis_size("tile")
    units_dev = visibility.shape[0]
    span = visibility.shape[4]
    slot_count = station_beam.shape[0]
    per_group = station_beam.shape[2]
    antennas = station_beam.shape[3]
    tile_index = lax.axis_index("tile")
    first_tab, second_tab, diag_tab = unit_table(BLOCKS)
    first_arr = jnp.asarray(first_tab)
    second_arr = jnp.asarray(second_tab)
    diag_arr = jnp.asarray(diag_tab)
    keep_all = 1.0 - antenna_flags.astype(jnp.float32)
    owned, brightness = build_factors(
        station_beam, antenna_uvw, source_dirs, source_flux, visible_list
    )
    gathered, bright_all = (
        lax.all_gather(owned, "tile", axis=2, tiled=True),
        lax.all_gather(brightness, "tile", axis=1, tiled=True),
    )
    residuals = []
    partial_total = jnp.zeros((slot_count, per_group * tile_count), jnp.float32)
    for unit_slot in range(units_dev):
        unit_id = tile_index * units_dev + unit_slot
        start_one = (first_arr[unit_id] * span).astype(jnp.int32)
        start_two = (second_arr[unit_id] * span).astype(jnp.int32)
        diag_tile = diag_arr[unit_id] == 1
        block_one = lax.dynamic_slice_in_dim(gathered, start_one, span, 3)
        block_two = lax.dynamic_slice_in_dim(gathered, start_two, span, 3)
        keep_one = lax.dynamic_slice_in_dim(keep_all, start_one, span, 1)
        keep_two = lax.dynamic_slice_in_dim(keep_all, start_two, span, 1)
        residual, partial_value = unit_work(
            block_one, block_two, diag_tile, bright_all, visibility[unit_slot], keep_one, keep_two
        )
        residuals.append(residual)
        partial_total = partial_total + partial_value
    summed = lax.psum_scatter(partial_total, "tile", scatter_dimension=1, tiled=True)
    flux_grad = summed * (-1.0 / (8.0 * antennas))
    return (jnp.stack(residuals, 0), flux_grad)


def solution(mesh):
    return jax.shard_map(
        per_device,
        mesh=mesh,
        in_specs=(
            P("tile", "grp", None, None, None),
            P("grp", None, "tile", None),
            P("grp", None, None),
            P(None, "tile"),
            P(("grp", "tile")),
            P(None, "tile"),
            P("grp", None),
        ),
        out_specs=(P("tile", "grp", None, None, None), P("grp", "tile")),
        check_vma=False,
    )
```

profile of v0, /device:TPU:0, one launch (start us, length us, event | category | flops | bytes accessed | tf_op | source)
XLA Modules:
  0.0 425.8 jit_solution(3471020011920112316)
XLA Ops:
  9.6 2.1 convert_element_type.106
  12.0 8.9 %add_convert_fusion = (bf16[8,1,32,2048]{3,2,1,0:T(8,128)(2,1)S(1)}, bf16[8,1,32,2048]{3,2,1,0:T(8,128)(2,1)S(1)}) fusion(f32[8,2,32,2048]{3,2,1,0:T(8,128)S(1)} %convert_element_type.106, f32[8,32]{1,0:T(8,128)S(1)} %sqrt_add_fusion, f32[8,2048]{1,0:T(8,128)S(1)} %get-tuple-element.134, f32[8,32]{1,0:T(8,128)S(1)} %get-tuple-element.95, ...), kind=kLoop, calls=%fused_computation.93 | loop fusion | flops 7340032 | bytes 6491136 | tf_op jit(solution)/shard_map/convert.2
  21.2 2.5 copy.115
  29.1 23.9 %all-gather = bf16[16,32,8]{1,2,0:T(8,128)(2,1)S(1)} all-gather(bf16[1,32,8]{1,2,0:T(8,128)(2,1)S(1)} %bitcast.185), channel_id=1, replica_groups=mesh['grp'=2,'tile'=16] {'tile'}, dimensions={0}, use_global_device_ids=true | all-gather | bytes 8704 | tf_op jit(solution)/shard_map/all_gather | solution.py:136
  53.4 2.7 multiply_select_fusion.1
  56.1 138.6 %all-gather.3.cloned.1.call-done = bf16[8,2,512,2048]{3,0,1,2:T(8,128)(2,1)} async-done(((bf16[8,2,32,2048]{3,0,1,2:T(8,128)(2,1)}), bf16[8,2,512,2048]{3,0,1,2:T(8,128)(2,1)}) %all-gather.3.cloned.1.call-update) | async-done | bytes 33554448 | tf_op jit(solution)/shard_map/all_gather | solution.py:135
  194.7 12.4 %constant_dynamic-slice_fusion.5 = (bf16[8,2,512,256]{3,0,1,2:T(8,128)(2,1)}, bf16[8,2,512,256]{3,0,1,2:T(8,128)(2,1)}, bf16[8,2,512,256]{3,0,1,2:T(8,128)(2,1)}, bf16[8,2,512,256]{3,0,1,2:T(8,128)(2,1)}) fusion(bf16[8,2,512,2048]{3,0,1,2:T(8,128)(2,1)} %all-gather.3.cloned.1.call-done, s32[]{:T(128)S(6)} %select_n.94, s32[]{:T(128)S(6)} %select_n.105, ...), kind=kLoop, calls=%fused_computation.123 | loop fusion | bytes 33554448 | tf_op jit(solution)/shard_map/dynamic_slice | solution.py:145
  207.1 7.6 %copy.167 = bf16[8,2,512,256]{2,3,1,0:T(8,128)(2,1)} copy(bf16[8,2,512,256]{3,0,1,2:T(8,128)(2,1)} %get-tuple-element.111) | data formatting | bytes 8388608
  214.7 7.6 %copy.169 = bf16[8,2,512,256]{2,3,1,0:T(8,128)(2,1)} copy(bf16[8,2,512,256]{3,0,1,2:T(8,128)(2,1)} %get-tuple-element.112) | data formatting | bytes 8388608
  222.3 7.5 %fusion.44 = (bf16[8,2,512,256]{2,3,1,0:T(8,128)(2,1)S(1)}, bf16[8,2,512,256]{2,3,1,0:T(8,128)(2,1)}) fusion(bf16[8,2,512,256]{2,3,1,0:T(8,128)(2,1)} %copy.167, f32[8,512]{1,0:T(8,128)S(1)} %bitcast_convert_fusion, bf16[8,2,512,256]{2,3,1,0:T(8,128)(2,1)} %copy.169), kind=kLoop, calls=%fused_computation.50 | loop fusion | flops 12582912 | bytes 16793600 | tf_op jit(solution)/shard_map/convert_element_type | solution.py:59
  229.8 1.9 fusion.91
  232.4 7.6 %copy.168 = bf16[8,2,512,256]{2,3,1,0:T(8,128)(2,1)} copy(bf16[8,2,512,256]{3,0,1,2:T(8,128)(2,1)} %get-tuple-element.113) | data formatting | bytes 8388608
  240.1 2.5 conditional.4
  240.1 2.5 broadcast.220
  242.5 5.4 %copy.121 = f32[8,2,256,256]{2,3,1,0:T(8,128)} copy(f32[8,2,256,256]{3,2,1,0:T(8,128)} %get-tuple-element.156) | data formatting | bytes 8388608 | tf_op jit(solution)/shard_map/cond | solution.py:83
  248.0 4.3 %maximum_bitcast_fusion.6 = bf16[8,1,2,512,256]{3,4,2,1,0:T(8,128)(2,1)} fusion(bf16[8,1,512,256]{2,3,1,0:T(8,128)(2,1)} %get-tuple-element.118, bf16[8,1,512,256]{2,3,1,0:T(8,128)(2,1)S(1)} %get-tuple-element.117), kind=kLoop, calls=%fused_computation.61 | loop fusion | flops 2097152 | bytes 8388608 | tf_op jit(solution)/shard_map/stack | solution.py:63
  253.6 8.4 %broadcast_select_fusion.3 = (bf16[8,2,256,256]{3,2,1,0:T(8,128)(2,1)S(1)}, bf16[8,2,256,256]{3,2,1,0:T(8,128)(2,1)}) fusion(pred[256,256]{1,0:T(8,128)(4,1)S(1)} %fusion.85, f32[8,2,256,256]{2,3,1,0:T(8,128)} %copy.121, bf16[8,2,512,256]{2,3,1,0:T(8,128)(2,1)S(1)} %copy-done.6, bf16[8,2,512,256]{2,3,1,0:T(8,128)(2,1)S(1)} %copy-done, pred[]{:T(512)} %bitcast.28, ...), kind=kOutput, calls=%fused_computation.99 | convolution fusion | flops 2160066560 | bytes 29425664 | tf_op jit(solution)/shard_map/tdckr,tckq->tdrq/dot_general | solution.py:64
  262.0 1.8 slice_negate_fusion.7
  265.3 1.6 fusion.92
  266.9 7.5 %copy.170 = bf16[8,2,512,256]{2,3,1,0:T(8,128)(2,1)} copy(bf16[8,2,512,256]{3,0,1,2:T(8,128)(2,1)} %get-tuple-element.114) | data formatting | bytes 8388608
  274.4 2.5 conditional.5
  274.4 2.5 broadcast.221
  276.9 5.3 %copy.126 = f32[8,2,256,256]{2,3,1,0:T(8,128)} copy(f32[8,2,256,256]{3,2,1,0:T(8,128)} %get-tuple-element.157) | data formatting | bytes 8388608 | tf_op jit(solution)/shard_map/cond | solution.py:83
  282.2 4.3 %maximum_bitcast_fusion.7 = bf16[8,1,2,512,256]{3,4,2,0,1:T(8,128)(2,1)} fusion(bf16[8,1,512,256]{2,3,1,0:T(8,128)(2,1)} %get-tuple-element.120, bf16[8,1,512,256]{2,3,1,0:T(8,128)(2,1)S(1)} %get-tuple-element.119), kind=kLoop, calls=%fused_computation.62 | loop fusion | flops 2097152 | bytes 8388608 | tf_op jit(solution)/shard_map/stack | solution.py:63
  287.8 8.8 %broadcast_select_fusion.2 = (bf16[8,2,256,256]{3,2,1,0:T(8,128)(2,1)S(1)}, bf16[8,2,256,256]{3,2,1,0:T(8,128)(2,1)}) fusion(pred[256,256]{1,0:T(8,128)(4,1)S(1)} %fusion.84, f32[8,2,256,256]{2,3,1,0:T(8,128)} %copy.126, bf16[8,2,512,256]{2,3,1,0:T(8,128)(2,1)S(1)} %copy-done.4, bf16[8,2,512,256]{2,3,1,0:T(8,128)(2,1)} %copy.170, pred[]{:T(512)} %bitcast.48, ...), kind=kOutput, calls=%fused_computation.98 | convolution fusion | flops 2160066560 | bytes 29425664 | tf_op jit(solution)/shard_map/tdckr,tckq->tdrq/dot_general | solution.py:64
  296.6 1.8 slice_negate_fusion.6
  299.6 4.5 %maximum_bitcast_fusion.8 = (bf16[8,1,2,256,256]{4,3,2,0,1:T(8,128)(2,1)}, bf16[8,1,2,256,256]{4,3,2,0,1:T(8,128)(2,1)}) fusion(bf16[8,1,256,256]{3,2,1,0:T(8,128)(2,1)S(1)} %copy-done.10, bf16[8,1,256,256]{3,2,1,0:T(8,128)(2,1)} %get-tuple-element.123, bf16[8,1,256,256]{3,2,1,0:T(8,128)(2,1)} %get-tuple-element.122), kind=kLoop, calls=%fused_computation.87 | loop fusion | flops 2097152 | bytes 7340032 | tf_op jit(solution)/shard_map/stack | solution.py:68
  304.2 6.4 %fusion.45 = f32[8,512]{1,0:T(8,128)S(1)} fusion(bf16[8,2,512,256]{2,3,1,0:T(8,128)(2,1)} %copy.167, bf16[8,2,512,256]{2,3,1,0:T(8,128)(2,1)S(1)} %copy-done.1, pred[]{:T(512)} %bitcast.28, bf16[8,1,2,256,256]{4,3,2,0,1:T(8,128)(2,1)} %get-tuple-element.128, bf16[8,1,2,256,256]{4,3,2,0,1:T(8,128)(2,1)} %get-tuple-element.127), kind=kOutput, calls=%fused_computation.51 | convolution fusion | flops 2157965312 | bytes 12599297 | tf_op jit(solution)/shard_map/tdcrq,tckq->tdkr/dot_general | solution.py:71
  310.7 4.1 maximum_bitcast_fusion.10
  314.8 6.4 %fusion.47 = f32[8,512]{1,0:T(8,128)S(1)} fusion(bf16[8,2,512,256]{2,3,1,0:T(8,128)(2,1)S(1)} %copy-done.5, bf16[8,2,512,256]{2,3,1,0:T(8,128)(2,1)} %copy.170, pred[]{:T(512)} %bitcast.48, bf16[8,1,2,256,256]{4,3,2,0,1:T(8,128)(2,1)} %get-tuple-element.130, bf16[8,1,2,256,256]{4,3,2,0,1:T(8,128)(2,1)} %get-tuple-element.129), kind=kOutput, calls=%fused_computation.53 | convolution fusion | flops 2157965312 | bytes 12599297 | tf_op jit(solution)/shard_map/tdcrq,tckq->tdkr/dot_general | solution.py:71
  322.4 4.6 %pad_maximum_fusion.1 = bf16[2,8,2,256,256]{4,3,2,1,0:T(8,128)(2,1)} fusion(bf16[1,8,2,256,256]{4,3,2,1,0:T(8,128)(2,1)} %bitcast.180, bf16[1,8,2,256,256]{4,3,2,1,0:T(8,128)(2,1)} %bitcast.179), kind=kLoop, calls=%fused_computation.63 | loop fusion | flops 2097152 | bytes 8388608 | tf_op jit(solution)/shard_map/stack | solution.py:156
  327.0 90.5 %reduce-scatter.4.cloned.1.call-done = f32[32,8]{1,0:T(8,128)} async-done(((f32[512,8]{1,0:T(8,128)}), f32[32,8]{1,0:T(8,128)}) %reduce-scatter.4.cloned.1.call-update) | async-done | bytes 1040
  (63 shorter events, 13.5 us)
Async XLA Ops:
  7.2 4.5 %copy-start.15 = (s32[8,32]{1,0:T(8,128)S(1)}, s32[8,32]{1,0:T(8,128)}, u32[]{:S(2)}) copy-start(s32[8,32]{1,0:T(8,128)} %param.23) | copy-start | bytes 3076
  7.2 187.5 %all-gather.3.cloned.1.call-start = ((), (), s32[]{:S(2)}) async-start(), calls=%async_computation.1 | async-start | bytes 35651584 | tf_op jit(solution)/shard_map/all_gather | solution.py:135
  21.1 2.6 copy-start.17
  21.2 2.6 copy-start.18
  21.2 5.9 %copy-start.16 = (s32[32]{0:T(128)S(1)}, s32[32]{0:T(128)}, u32[]{:S(2)}) copy-start(s32[32]{0:T(128)} %constant.62.clone) | copy-start | bytes 388
  21.2 32.1 %copy-start.14 = (s32[8,2048]{1,0:T(8,128)S(1)}, s32[8,2048]{1,0:T(8,128)}, u32[]{:S(2)}) copy-start(s32[8,2048]{1,0:T(8,128)} %param.24) | copy-start | bytes 196612
  23.7 393.8 %reduce-scatter.4.cloned.1.call-start = ((), (), s32[]{:S(2)}) async-start(), calls=%async_computation.2 | async-start | bytes 278528
  229.8 2.7 copy-start.9
  248.0 4.3 %copy-start = (bf16[8,2,512,256]{2,3,1,0:T(8,128)(2,1)S(1)}, bf16[8,2,512,256]{2,3,1,0:T(8,128)(2,1)}, u32[]{:S(2)}) copy-start(bf16[8,2,512,256]{2,3,1,0:T(8,128)(2,1)} %copy.168) | copy-start | bytes 12582916
  248.0 5.6 %copy-start.6 = (bf16[8,2,512,256]{2,3,1,0:T(8,128)(2,1)S(1)}, bf16[8,2,512,256]{2,3,1,0:T(8,128)(2,1)}, u32[]{:S(2)}) copy-start(bf16[8,2,512,256]{2,3,1,0:T(8,128)(2,1)} %copy.167) | copy-start | bytes 12582916
  262.0 3.3 copy-start.7
  282.2 4.3 %copy-start.4 = (bf16[8,2,512,256]{2,3,1,0:T(8,128)(2,1)S(1)}, bf16[8,2,512,256]{2,3,1,0:T(8,128)(2,1)}, u32[]{:S(2)}) copy-start(bf16[8,2,512,256]{2,3,1,0:T(8,128)(2,1)} %copy.169) | copy-start | bytes 12582916
  282.2 5.6 %copy-start.8 = (bf16[8,2,512,256]{2,3,1,0:T(8,128)(2,1)S(1)}, bf16[8,2,512,256]{2,3,1,0:T(8,128)(2,1)}, u32[]{:S(2)}) copy-start(bf16[8,2,512,256]{2,3,1,0:T(8,128)(2,1)} %get-tuple-element.141) | copy-start | bytes 12582916
  298.4 1.2 copy-start.10
  298.4 5.8 %copy-start.1 = (bf16[8,2,512,256]{2,3,1,0:T(8,128)(2,1)S(1)}, bf16[8,2,512,256]{2,3,1,0:T(8,128)(2,1)}, u32[]{:S(2)}) copy-start(bf16[8,2,512,256]{2,3,1,0:T(8,128)(2,1)} %copy.168) | copy-start | bytes 12582916
  304.2 6.5 %copy-start.11 = (bf16[8,1,256,256]{3,2,1,0:T(8,128)(2,1)S(1)}, bf16[8,1,256,256]{3,2,1,0:T(8,128)(2,1)}, u32[]{:S(2)}) copy-start(bf16[8,1,256,256]{3,2,1,0:T(8,128)(2,1)} %get-tuple-element.124) | copy-start | bytes 3145732
  304.2 6.5 %copy-start.12 = (bf16[8,1,256,256]{3,2,1,0:T(8,128)(2,1)S(1)}, bf16[8,1,256,256]{3,2,1,0:T(8,128)(2,1)}, u32[]{:S(2)}) copy-start(bf16[8,1,256,256]{3,2,1,0:T(8,128)(2,1)} %get-tuple-element.125) | copy-start | bytes 3145732
  310.6 4.2 copy-start.5
Sparse Core Ops, SparseCore 0:
  23.8 170.8 all-gather.2
  322.5 94.9 reduce-scatter.3
where the time goes:
time: 427 us; the launch traced here: 426 us
  waiting for transfers between devices  229 us (54%)
  local copies, waits for them, and re-layouts  72.1 us (17%)
  other arithmetic  52 us (12%)
  matrix products  30 us (7%)
  blocking collectives  23.9 us (6%)
  between operations  18.3 us (4%)
    all_gather x1, waiting for transfers between devices, per_device(): lax.all_gather(owned, 'tile', axis=2, tiled=True)  139 us
    unnamed x3, waiting for transfers between devices  90.5 us
    unnamed x39, local copies, waits for them, and re-layouts  38.4 us
    all_gather x1, blocking collectives, per_device(): lax.all_gather(brightness, 'tile', axis=1, tiled=True)  23.9 us
    dot_general x2, matrix products, predict(): jnp.einsum('tdckr,tckq->tdrq', stacked, cols_f, preferred_element_type=jn...  17.2 us
    dot_general x2, matrix products, pull_back(): jnp.einsum('tdcrq,tckq->tdkr', rstack, cols_f, preferred_element_type=jnp...  12.9 us
    dynamic_slice x1, local copies, waits for them, and re-layouts, per_device(): block_one = lax.dynamic_slice_in_dim(gathered, start_one, span, 3)  12.4 us
    cond x2, local copies, waits for them, and re-layouts, unit_work(): lax.cond(diag_tile, lambda: predict(block_two, block_two, bright_all), la...  10.8 us
  transfers between devices with their start and end apart: 2, of which 2 were waited for; matrix products, arithmetic and copies ran while one was open for 2% of the time, Pallas kernels for 0%

commit v1 on v0

v1 whole, which is shorter than its diff:
```python
import functools
import math

import jax
import jax.numpy as jnp
from jax import lax
from jax.experimental import pallas as pl
from jax.experimental.pallas import tpu as pltpu
from jax.sharding import PartitionSpec as P

BLOCKS = 8
MESH = pl.DeviceIdType.MESH

two_pi = 2.0 * math.pi


def build_factors(station_beam, antenna_uvw, source_dirs, source_flux, visible_list):
    pool_size = source_dirs.shape[1]
    slots, _, per_group, antennas = station_beam.shape
    span = antennas // BLOCKS
    chosen = visible_list[:, :, None] == jnp.arange(pool_size, dtype=jnp.int32)[None, None, :]
    coord_east = jnp.sum(jnp.where(chosen, source_dirs[0][None, None, :], 0.0), axis=2)
    coord_north = jnp.sum(jnp.where(chosen, source_dirs[1][None, None, :], 0.0), axis=2)
    brightness = jnp.sum(
        jnp.where(chosen, source_flux.astype(jnp.float32)[None, None, :], 0.0), axis=2
    ).astype(jnp.bfloat16)
    depth_term = jnp.sqrt(1.0 - coord_east * coord_east - coord_north * coord_north) - 1.0
    delay_sum = (
        antenna_uvw[:, 0, None, :] * coord_east[:, :, None]
        + antenna_uvw[:, 1, None, :] * coord_north[:, :, None]
        + antenna_uvw[:, 2, None, :] * depth_term[:, :, None]
    )
    phases = two_pi * delay_sum
    cosine = jnp.cos(phases)
    sine = jnp.sin(phases)
    beam_f = station_beam.astype(jnp.float32)
    real_part = beam_f[:, 0] * cosine + beam_f[:, 1] * sine
    imag_part = beam_f[:, 1] * cosine - beam_f[:, 0] * sine
    both = jnp.stack([real_part, imag_part], 1).astype(jnp.bfloat16)
    both = both.reshape(slots, 2, per_group, BLOCKS, span).transpose(0, 3, 1, 2, 4)
    return both.reshape(slots, BLOCKS, 2 * per_group, span), brightness


def unit_blocks(unit_id):
    pairs = BLOCKS * (BLOCKS - 1) // 2
    first = jnp.int32(0)
    start = jnp.int32(0)
    offset = 0
    for row in range(1, BLOCKS - 1):
        offset += BLOCKS - row
        first = jnp.where(unit_id >= offset, jnp.int32(row), first)
        start = jnp.where(unit_id >= offset, jnp.int32(offset), start)
    second = unit_id - start + first + 1
    diag = unit_id >= pairs
    first = jnp.where(diag, 2 * (unit_id - pairs), first)
    second = jnp.where(diag, 2 * (unit_id - pairs) + 1, second)
    return first, second, diag


def kernel(
    dims, own, bright, keep, vis, res, flux,
    gath, ball, work, flx, frecv,
    r_sem, su, sd, sy, sc, lc, vsem, osem, bs, br, fs, fr,
):
    Z, Y, slots, units, per_group, span, scale = dims
    T = Z * Y * 2
    me = lax.axis_index("tile")
    core = me % 2
    y = (me // 2) % Y
    z = me // (2 * Y)

    def dev(zi, yi, ci):
        return (zi * Y + yi) * 2 + ci

    other = dev(z, y, 1 - core)
    yother = (y + 1) % Y

    def rc(src, s, sh, target, sem):
        return pltpu.make_async_remote_copy(
            src_ref=src, dst_ref=gath.at[s, :, sh], send_sem=sem, recv_sem=r_sem.at[s, sh],
            device_id={"tile": target}, device_id_type=MESH,
        )

    def arrived(s, sh):
        rc(gath.at[s, :, sh], s, sh, other, lc.at[s]).wait_recv()

    def small(src, dst, send, recv, target):
        return pltpu.make_async_remote_copy(
            src_ref=src, dst_ref=dst, send_sem=send, recv_sem=recv,
            device_id={"tile": target}, device_id_type=MESH,
        )

    def each(body, count):
        def step(i, carry):
            body(i)
            return carry
        lax.fori_loop(0, count, step, 0)

    def vis_copy(s, u):
        return pltpu.make_async_copy(vis.at[u, s], work.at[s, u], vsem.at[s, u])

    def res_copy(s, u):
        return pltpu.make_async_copy(work.at[s, u], res.at[u, s], osem.at[s, u])

    barrier = pltpu.get_barrier_semaphore()
    each(lambda k: pl.semaphore_signal(
        barrier, inc=1, device_id={"tile": (me + k + 1) % T}, device_id_type=MESH), T - 1)
    pl.semaphore_wait(barrier, T - 1)

    def up(src, s, zi):
        return rc(src, s, dev(zi, y, core), dev(z + 1, y, core), su.at[s, zi])

    def down(src, s, zi):
        return rc(src, s, dev(zi, y, core), dev(z - 1, y, core), sd.at[s, zi])

    def across(src, s, zi):
        return rc(src, s, dev(zi, y, core), dev(z, yother, core), sy.at[s, zi])

    def mate(src, s, zi, yi):
        return rc(src, s, dev(zi, yi, core), other, sc.at[s, zi * Y + yi])

    def own_step(s):
        src = own.at[s]

        @pl.when(z < Z - 1)
        def _():
            up(src, s, z).start()

        @pl.when(z > 0)
        def _():
            down(src, s, z).start()

        if Y > 1:
            across(src, s, z).start()
        mate(src, s, z, y).start()
        pltpu.make_async_copy(src, gath.at[s, :, me], lc.at[s]).start()

    each(own_step, slots)

    def bright_step(k):
        target = (me + k + 1) % T
        small(bright, ball.at[me], bs.at[k], br.at[me], target).start()
    each(bright_step, T - 1)
    ball[me] = bright[...]

    def vis_step(s):
        for u in range(units):
            vis_copy(s, u).start()
    each(vis_step, slots)
    flx[...] = jnp.zeros_like(flx)

    def z_step(d, s):
        @pl.when(z - d >= 0)
        def _():
            zi = z - d
            sh = dev(zi, y, core)
            arrived(s, sh)
            src = gath.at[s, :, sh]

            @pl.when(z < Z - 1)
            def _():
                up(src, s, zi).start()
            if Y > 1:
                across(src, s, zi).start()
            mate(src, s, zi, y).start()

        @pl.when(z + d < Z)
        def _():
            zi = z + d
            sh = dev(zi, y, core)
            arrived(s, sh)
            src = gath.at[s, :, sh]

            @pl.when(z > 0)
            def _():
                down(src, s, zi).start()
            if Y > 1:
                across(src, s, zi).start()
            mate(src, s, zi, y).start()

    def y_one(zi, s):
        sh = dev(zi, yother, core)
        arrived(s, sh)
        mate(gath.at[s, :, sh], s, zi, yother).start()

    def y_step(d, s):
        if Y == 1:
            return
        if d == 0:
            y_one(z, s)
            return
        pl.when(z - d >= 0)(lambda: y_one(z - d, s))
        pl.when(z + d < Z)(lambda: y_one(z + d, s))

    def hop_step(d, s):
        z_step(d, s)
        y_step(d - 1, s)

    for d in range(1, Z):
        each(functools.partial(hop_step, d), slots)

    def bright_wait(k):
        src = (me + k + 1) % T
        small(bright, ball.at[src], bs.at[k], br.at[src], other).wait_recv()
    each(bright_wait, T - 1)

    rows = T * 2 * per_group
    split = (T, 2, per_group, span)

    def turn(a):
        a4 = a.reshape(split)
        return jnp.concatenate([a4[:, 1:], -a4[:, :1]], axis=1).reshape(rows, span)

    def tn(a, b):
        return lax.dot_general(a, b, (((0,), (0,)), ((), ())), preferred_element_type=jnp.float32)

    def nt(a, b):
        return lax.dot_general(a, b, (((1,), (1,)), ((), ())), preferred_element_type=jnp.float32)

    def nn(a, b):
        return lax.dot_general(a, b, (((1,), (0,)), ((), ())), preferred_element_type=jnp.float32)

    def compute(s):
        lane = lax.broadcasted_iota(jnp.int32, (T, per_group, 128), 2)
        here = lane == s
        bcol = jnp.sum(jnp.where(here, ball[...].astype(jnp.float32), 0.0), axis=2, keepdims=True)

        def block(b):
            return gath[s, b].reshape(rows, span)

        def scaled_of(f):
            f4 = f.reshape(split).astype(jnp.float32)
            return (f4 * bcol[:, None]).astype(jnp.bfloat16).reshape(rows, span)

        def flag_rows(b):
            return jnp.broadcast_to(keep[s, b], (span, span)).T

        def add_flux(x, u, v):
            w = x.astype(jnp.float32) * u + turn(x).astype(jnp.float32) * v
            w = w.reshape(split)
            w = jnp.sum(w, axis=1)
            total = jnp.sum(w, axis=2, keepdims=True)
            flx[...] += jnp.where(here, total, 0.0)

        for u in range(units):
            p, q, diag = unit_blocks(me * units + u)
            vis_copy(s, u).wait()

            @pl.when(jnp.logical_not(diag))
            def _():
                x = block(p)
                c = block(q)
                sx = scaled_of(x)
                w = flag_rows(p) * keep[s, q]
                rre = (w * (work[s, u, 0].astype(jnp.float32) - tn(sx, c))).astype(jnp.bfloat16)
                rim = (w * (work[s, u, 1].astype(jnp.float32) - tn(turn(sx), c))).astype(jnp.bfloat16)
                work[s, u, 0] = rre
                work[s, u, 1] = rim
                add_flux(x, nt(c, rre), nt(c, rim))

            @pl.when(diag)
            def _():
                x = block(p)
                c = block(q)
                rid = lax.broadcasted_iota(jnp.int32, (span, span), 0)
                cid = lax.broadcasted_iota(jnp.int32, (span, span), 1)
                hi = rid < cid
                lo = rid > cid
                sx = scaled_of(x)
                sb = scaled_of(c)
                pre = jnp.where(hi, tn(sx, x), tn(c, sb))
                pim = jnp.where(hi, tn(turn(sx), x), tn(c, turn(sb)))
                w = jnp.where(hi, flag_rows(p) * keep[s, p], 0.0) + jnp.where(
                    lo, flag_rows(q) * keep[s, q], 0.0)
                rre = (w * (work[s, u, 0].astype(jnp.float32) - pre)).astype(jnp.bfloat16)
                rim = (w * (work[s, u, 1].astype(jnp.float32) - pim)).astype(jnp.bfloat16)
                work[s, u, 0] = rre
                work[s, u, 1] = rim
                zero = jnp.zeros((span, span), jnp.float32)
                def part(r, m):
                    return jnp.where(m, r.astype(jnp.float32), zero).astype(jnp.bfloat16)
                add_flux(x, nt(x, part(rre, hi)), nt(x, part(rim, hi)))
                add_flux(c, nn(c, part(rre, lo)), nn(c, part(rim, lo)))

            res_copy(s, u).start()


    def last_step(s):
        y_step(Z - 1, s)
        pltpu.make_async_copy(own.at[s], gath.at[s, :, me], lc.at[s]).wait()
        for i in range(T // 2):
            arrived(s, 2 * i + 1 - core)
        compute(s)

    each(last_step, slots)

    def flux_step(k):
        target = (me + k + 1) % T
        small(flx.at[target], frecv.at[me], fs.at[k], fr.at[me], target).start()
    each(flux_step, T - 1)
    frecv[me] = flx[me]

    def tidy(s):
        for u in range(units):
            res_copy(s, u).wait()
        for zi in range(Z):
            pl.when(jnp.logical_and(zi <= z, z < Z - 1))(lambda: up(own.at[s], s, zi).wait_send())
            pl.when(jnp.logical_and(zi >= z, z > 0))(lambda: down(own.at[s], s, zi).wait_send())
            if Y > 1:
                across(own.at[s], s, zi).wait_send()
            for yi in range(Y):
                mate(own.at[s], s, zi, yi).wait_send()
    each(tidy, slots)

    def small_wait(k):
        src = (me + k + 1) % T
        small(bright, ball.at[me], bs.at[k], br.at[me], src).wait_send()
        one = small(flx.at[src], frecv.at[src], fs.at[k], fr.at[src], src)
        one.wait_send()
        one.wait_recv()
    each(small_wait, T - 1)
    flux[...] = jnp.sum(frecv[...], axis=0) * scale


def per_device(
    layout, visibility, station_beam, antenna_uvw, source_dirs, source_flux, visible_list, antenna_flags
):
    Z, Y = layout
    T = lax.axis_size("tile")
    units, slots, _, span, _ = visibility.shape
    per_group = station_beam.shape[2]
    antennas = station_beam.shape[3]
    keep_all = 1.0 - antenna_flags.astype(jnp.float32)
    keep_all = keep_all.reshape(slots, BLOCKS, 1, span)
    own, brightness = build_factors(
        station_beam, antenna_uvw, source_dirs, source_flux, visible_list
    )
    bright = jnp.pad(brightness.T, ((0, 0), (0, 128 - slots)))
    dims = (Z, Y, slots, units, per_group, span, -1.0 / (8.0 * antennas))
    vmem = pl.BlockSpec(memory_space=pltpu.VMEM)
    hbm = pl.BlockSpec(memory_space=pl.ANY)
    dma = pltpu.SemaphoreType.DMA
    residual, flux = pl.pallas_call(
        functools.partial(kernel, dims),
        name="predict_pull",
        out_shape=(
            jax.ShapeDtypeStruct(visibility.shape, jnp.bfloat16),
            jax.ShapeDtypeStruct((per_group, 128), jnp.float32),
        ),
        in_specs=[vmem, vmem, vmem, hbm],
        out_specs=(hbm, vmem),
        scratch_shapes=[
            pltpu.VMEM((slots, BLOCKS, T, 2 * per_group, span), jnp.bfloat16),
            pltpu.VMEM((T, per_group, 128), jnp.bfloat16),
            pltpu.VMEM((slots, units, 2, span, span), jnp.bfloat16),
            pltpu.VMEM((T, per_group, 128), jnp.float32),
            pltpu.VMEM((T, per_group, 128), jnp.float32),
            dma((slots, T)),
            dma((slots, Z)),
            dma((slots, Z)),
            dma((slots, Z)),
            dma((slots, Z * Y)),
            dma((slots,)),
            dma((slots, units)),
            dma((slots, units)),
            dma((T,)),
            dma((T,)),
            dma((T,)),
            dma((T,)),
        ],
        compiler_params=pltpu.CompilerParams(
            collective_id=0, has_side_effects=True, vmem_limit_bytes=64 * 1024 * 1024 - 2 * 65536
        ),
    )(own, bright, keep_all, visibility)
    return residual, flux[:, :slots].T


def layout_of(mesh):
    count = mesh.shape["tile"]
    line = mesh.devices.reshape(-1, count)[0]
    places = [getattr(d, "coords", None) for d in line]
    fast = 1
    if all(c is not None for c in places):
        fast = max(1, len({tuple(c)[1] for c in places}))
    if (count // 2) % fast or fast > 2:
        fast = 1
    return count // 2 // fast, fast


def solution(mesh):
    return jax.shard_map(
        functools.partial(per_device, layout_of(mesh)),
        mesh=mesh,
        in_specs=(
            P("tile", "grp", None, None, None),
            P("grp", None, "tile", None),
            P("grp", None, None),
            P(None, "tile"),
            P(("grp", "tile")),
            P(None, "tile"),
            P("grp", None),
        ),
        out_specs=(P("tile", "grp", None, None, None), P("grp", "tile")),
        check_vma=False,
    )
```

time: 427 us -> 242 us (0.57)
  waiting for transfers between devices: 229 us -> 0 us
  Pallas kernels: 0 us -> 216 us
  local copies, waits for them, and re-layouts: 72.1 us -> 10.2 us
  other arithmetic: 52 us -> 15 us
  matrix products: 30 us -> 0 us
  blocking collectives: 23.9 us -> 0 us
  between operations: 18.3 us -> 0.7 us
    pallas_call x0 -> x1, Pallas kernels: none -> 216 us  [per_device(): pl.pallas_call(functools.partial(kernel, dims), name='predict_pull', out_...]
    all_gather x1 -> x0, waiting for transfers between devices: 139 us -> none  [per_device(): lax.all_gather(owned, 'tile', axis=2, tiled=True)]
    unnamed x3 -> x0, waiting for transfers between devices: 90.5 us -> none
    unnamed x39 -> x4, local copies, waits for them, and re-layouts: 38.4 us -> 5.9 us
    dot_general x4 -> x0, matrix products: 30 us -> none  [the longest x2 17.2 us: predict(): jnp.einsum('tdckr,tckq->tdrq', stacked, cols_f, preferred_element_type=jn...]
    all_gather x1 -> x0, blocking collectives: 23.9 us -> none  [per_device(): lax.all_gather(brightness, 'tile', axis=1, tiled=True)]
    another operation x7 -> x2, other arithmetic: 31 us -> 10.5 us
    dynamic_slice x4 -> x0, local copies, waits for them, and re-layouts: 13.8 us -> none  [the longest x1 12.4 us: per_device(): block_one = lax.dynamic_slice_in_dim(gathered, start_one, span, 3)]
  transfers between devices with their start and end apart: 2 -> 0, of which waited for: 2 -> 0; matrix products, arithmetic and copies ran while one was open for 2% -> 0% of each run, Pallas kernels for 0% -> 0%
where the time goes in v1:
time: 242 us
  Pallas kernels  216 us (89%)
  other arithmetic  15 us (6%)
  local copies, waits for them, and re-layouts  10.2 us (4%)
    pallas_call x1, Pallas kernels, per_device(): pl.pallas_call(functools.partial(kernel, dims), name='predict_pull', out_...  216 us
    another operation x1, other arithmetic  8.95 us
    unnamed x4, local copies, waits for them, and re-layouts  5.9 us

profile of v1, /device:TPU:0, one launch (start us, length us, event | category | flops | bytes accessed | tf_op | source)
XLA Modules:
  0.0 241.9 jit_solution(16566715868581586906)
XLA Ops:
  0.6 0.7 convert_element_type.21
  1.3 0.8 fusion.2
  2.0 1.0 select_reduce_fusion
  3.0 0.1 copy.18
  3.1 0.6 pad.4.bright
  3.7 0.8 convert_subtract_fusion
  4.6 0.7 reshape.56.keep
  5.3 0.9 slice_bitcast_fusion.2
  6.2 2.1 convert_element_type.20
  8.3 8.9 %add_convert_fusion = (bf16[8,1,32,2048]{3,2,1,0:T(8,128)(2,1)S(1)}, bf16[8,1,32,2048]{3,2,1,0:T(8,128)(2,1)S(1)}) fusion(f32[8,2,32,2048]{3,2,1,0:T(8,128)S(1)} %convert_element_type.20, f32[8,32]{1,0:T(8,128)S(1)} %sqrt_add_fusion, f32[8,2048]{1,0:T(8,128)S(1)} %get-tuple-element.18, f32[8,32]{1,0:T(8,128)S(1)} %get-tuple-element.13, ...), kind=kLoop, calls=%fused_computation.2 | loop fusion | flops 7340032 | bytes 6491136 | tf_op jit(solution)/shard_map/convert.3
  17.3 0.3 copy.20
  17.6 0.3 copy.16
  17.8 0.3 copy.21
  18.2 0.3 copy.17
  18.4 1.5 pad_maximum_fusion
  19.9 216.0 %predict_pull.1 = (bf16[2,8,2,256,256]{4,3,2,1,0:T(8,128)(2,1)}, f32[32,128]{1,0:T(8,128)}) custom-call(bf16[8,8,64,256]{3,2,1,0:T(8,128)(2,1)} %bitcast.26, bf16[32,128]{1,0:T(8,128)(2,1)} %pad.4.bright, f32[8,8,1,256]{3,2,1,0:T(1,128)} %reshape.56.keep, bf16[2,8,2,256,256]{4,3,2,1,0:T(8,128)(2,1)} %vis.1), custom_call_target="tpu_custom_call" | custom-call | tf_op jit(solution)/shard_map/predict_pull/pallas_call | solution.py:343
  235.9 0.7 slice_bitcast_fusion.3
  236.6 0.7 copy.19
  237.3 4.6 %copy.23 = bf16[2,8,2,256,256]{4,3,2,1,0:T(8,128)(2,1)} copy(bf16[2,8,2,256,256]{4,3,2,1,0:T(8,128)(2,1)} %get-tuple-element.24) | data formatting | bytes 8388608
  (1 shorter events, 0.0 us)

commit v2 on v1

--- a/solution.py
+++ b/solution.py
@@ -14,31 +14,19 @@
 two_pi = 2.0 * math.pi
 
 
-def build_factors(station_beam, antenna_uvw, source_dirs, source_flux, visible_list):
-    pool_size = source_dirs.shape[1]
-    slots, _, per_group, antennas = station_beam.shape
-    span = antennas // BLOCKS
-    chosen = visible_list[:, :, None] == jnp.arange(pool_size, dtype=jnp.int32)[None, None, :]
-    coord_east = jnp.sum(jnp.where(chosen, source_dirs[0][None, None, :], 0.0), axis=2)
-    coord_north = jnp.sum(jnp.where(chosen, source_dirs[1][None, None, :], 0.0), axis=2)
-    brightness = jnp.sum(
-        jnp.where(chosen, source_flux.astype(jnp.float32)[None, None, :], 0.0), axis=2
-    ).astype(jnp.bfloat16)
-    depth_term = jnp.sqrt(1.0 - coord_east * coord_east - coord_north * coord_north) - 1.0
-    delay_sum = (
-        antenna_uvw[:, 0, None, :] * coord_east[:, :, None]
-        + antenna_uvw[:, 1, None, :] * coord_north[:, :, None]
-        + antenna_uvw[:, 2, None, :] * depth_term[:, :, None]
-    )
-    phases = two_pi * delay_sum
-    cosine = jnp.cos(phases)
-    sine = jnp.sin(phases)
-    beam_f = station_beam.astype(jnp.float32)
-    real_part = beam_f[:, 0] * cosine + beam_f[:, 1] * sine
-    imag_part = beam_f[:, 1] * cosine - beam_f[:, 0] * sine
-    both = jnp.stack([real_part, imag_part], 1).astype(jnp.bfloat16)
-    both = both.reshape(slots, 2, per_group, BLOCKS, span).transpose(0, 3, 1, 2, 4)
-    return both.reshape(slots, BLOCKS, 2 * per_group, span), brightness
+def sin_cos_turns(turns):
+    quarter = jnp.floor(turns * 4.0 + 0.5)
+    angle = two_pi * (turns - quarter * 0.25)
+    a2 = angle * angle
+    sn = angle * (1.0 + a2 * (-1.0 / 6 + a2 * (1.0 / 120 + a2 * (-1.0 / 5040 + a2 * (1.0 / 362880)))))
+    cs = 1.0 + a2 * (-0.5 + a2 * (1.0 / 24 + a2 * (-1.0 / 720 + a2 * (1.0 / 40320 - a2 * (1.0 / 3628800)))))
+    kind = quarter - 4.0 * jnp.floor(quarter * 0.25)
+    odd = jnp.logical_or(kind == 1.0, kind == 3.0)
+    sine = jnp.where(odd, cs, sn)
+    cosine = jnp.where(odd, sn, cs)
+    sine = jnp.where(kind >= 2.0, -sine, sine)
+    cosine = jnp.where(jnp.logical_or(kind == 1.0, kind == 2.0), -cosine, cosine)
+    return sine, cosine
 
 
 def unit_blocks(unit_id):
@@ -58,8 +46,8 @@
 
 
 def kernel(
-    dims, own, bright, keep, vis, res, flux,
-    gath, ball, work, flx, frecv,
+    dims, beam, uvw, dirs, pool_flux, listed, flags, vis, res, flux,
+    own, bacc, bright, gath, ball, work, flx, frecv,
     r_sem, su, sd, sy, sc, lc, vsem, osem, bs, br, fs, fr,
 ):
     Z, Y, slots, units, per_group, span, scale = dims
@@ -73,6 +61,7 @@
         return (zi * Y + yi) * 2 + ci
 
     other = dev(z, y, 1 - core)
+    early = slots // 8 if Y > 1 else 0
     yother = (y + 1) % Y
 
     def rc(src, s, sh, target, sem):
@@ -105,13 +94,19 @@
     barrier = pltpu.get_barrier_semaphore()
     each(lambda k: pl.semaphore_signal(
         barrier, inc=1, device_id={"tile": (me + k + 1) % T}, device_id_type=MESH), T - 1)
-    pl.semaphore_wait(barrier, T - 1)
-
-    def up(src, s, zi):
-        return rc(src, s, dev(zi, y, core), dev(z + 1, y, core), su.at[s, zi])
-
-    def down(src, s, zi):
-        return rc(src, s, dev(zi, y, core), dev(z - 1, y, core), sd.at[s, zi])
+
+    def up(src, s, zi, yi):
+        return rc(src, s, dev(zi, yi, core), dev(z + 1, y, core), su.at[s, zi * Y + yi])
+
+    def down(src, s, zi, yi):
+        return rc(src, s, dev(zi, yi, core), dev(z - 1, y, core), sd.at[s, zi * Y + yi])
+
+    def onward(s, zi, yi, upward, downward):
+        src = gath.at[s, :, dev(zi, yi, core)]
+        if upward:
+            pl.when(z < Z - 1)(lambda: up(src, s, zi, yi).start())
+        if downward:
+            pl.when(z > 0)(lambda: down(src, s, zi, yi).start())
 
     def across(src, s, zi):
         return rc(src, s, dev(zi, y, core), dev(z, yother, core), sy.at[s, zi])
@@ -124,18 +119,53 @@
 
         @pl.when(z < Z - 1)
         def _():
-            up(src, s, z).start()
+            up(src, s, z, y).start()
 
         @pl.when(z > 0)
         def _():
-            down(src, s, z).start()
+            down(src, s, z, y).start()
 
         if Y > 1:
             across(src, s, z).start()
         mate(src, s, z, y).start()
         pltpu.make_async_copy(src, gath.at[s, :, me], lc.at[s]).start()
 
-    each(own_step, slots)
+    pool_size = dirs.shape[1]
+    slot_lane = lax.broadcasted_iota(jnp.int32, (per_group, 128), 1)
+    pool_lane = lax.broadcasted_iota(jnp.int32, (per_group, pool_size), 1).astype(jnp.float32)
+
+    def make_factors(s):
+        at_slot = slot_lane == s
+        index = jnp.sum(jnp.where(at_slot, listed[...], 0.0), axis=1, keepdims=True)
+        chosen = pool_lane == index
+
+        def pick(row):
+            return jnp.sum(jnp.where(chosen, row, 0.0), axis=1, keepdims=True)
+
+        east = pick(dirs[0:1, :])
+        north = pick(dirs[1:2, :])
+        bacc[...] += jnp.where(at_slot, pick(pool_flux[...]), 0.0)
+        depth = jnp.sqrt(1.0 - east * east - north * north) - 1.0
+        for b in range(BLOCKS):
+            cut = slice(b * span, (b + 1) * span)
+            turns = uvw[s, 0:1, cut] * east + uvw[s, 1:2, cut] * north + uvw[s, 2:3, cut] * depth
+            sine, cosine = sin_cos_turns(turns)
+            b0 = beam[s, 0, :, cut].astype(jnp.float32)
+            b1 = beam[s, 1, :, cut].astype(jnp.float32)
+            own[s, b, :per_group] = (b0 * cosine + b1 * sine).astype(jnp.bfloat16)
+            own[s, b, per_group:] = (b1 * cosine - b0 * sine).astype(jnp.bfloat16)
+
+    bacc[...] = jnp.zeros_like(bacc)
+    make_factors(0)
+    pl.semaphore_wait(barrier, T - 1)
+
+    def make_and_send(s):
+        make_factors(s + 1)
+        own_step(s)
+    each(make_and_send, slots - 1)
+    bright[...] = bacc[...].astype(jnp.bfloat16)
+    flx[...] = jnp.zeros_like(flx)
+    own_step(slots - 1)
 
     def bright_step(k):
         target = (me + k + 1) % T
@@ -147,50 +177,34 @@
         for u in range(units):
             vis_copy(s, u).start()
     each(vis_step, slots)
-    flx[...] = jnp.zeros_like(flx)
+
+    def z_one(zi, s, upward):
+        sh = dev(zi, y, core)
+        arrived(s, sh)
+        onward(s, zi, y, upward, not upward)
+        if Y > 1:
+            pl.when(s >= early)(lambda: across(gath.at[s, :, sh], s, zi).start())
+        mate(gath.at[s, :, sh], s, zi, y).start()
 
     def z_step(d, s):
-        @pl.when(z - d >= 0)
-        def _():
-            zi = z - d
-            sh = dev(zi, y, core)
-            arrived(s, sh)
-            src = gath.at[s, :, sh]
-
-            @pl.when(z < Z - 1)
-            def _():
-                up(src, s, zi).start()
-            if Y > 1:
-                across(src, s, zi).start()
-            mate(src, s, zi, y).start()
-
-        @pl.when(z + d < Z)
-        def _():
-            zi = z + d
-            sh = dev(zi, y, core)
-            arrived(s, sh)
-            src = gath.at[s, :, sh]
-
-            @pl.when(z > 0)
-            def _():
-                down(src, s, zi).start()
-            if Y > 1:
-                across(src, s, zi).start()
-            mate(src, s, zi, y).start()
-
-    def y_one(zi, s):
+        pl.when(z - d >= 0)(lambda: z_one(z - d, s, True))
+        pl.when(z + d < Z)(lambda: z_one(z + d, s, False))
+
+    def y_one(zi, s, upward, downward):
         sh = dev(zi, yother, core)
         arrived(s, sh)
+        if early:
+            pl.when(s < early)(lambda: onward(s, zi, yother, upward, downward))
         mate(gath.at[s, :, sh], s, zi, yother).start()
 
     def y_step(d, s):
         if Y == 1:
             return
         if d == 0:
-            y_one(z, s)
+            y_one(z, s, True, True)
             return
-        pl.when(z - d >= 0)(lambda: y_one(z - d, s))
-        pl.when(z + d < Z)(lambda: y_one(z + d, s))
+        pl.when(z - d >= 0)(lambda: y_one(z - d, s, True, False))
+        pl.when(z + d < Z)(lambda: y_one(z + d, s, False, True))
 
     def hop_step(d, s):
         z_step(d, s)
@@ -232,8 +246,12 @@
             f4 = f.reshape(split).astype(jnp.float32)
             return (f4 * bcol[:, None]).astype(jnp.bfloat16).reshape(rows, span)
 
+        def keep_row(t, b):
+            start = pl.multiple_of(b * span, span)
+            return 1.0 - flags[pl.ds(t, 1), pl.ds(start, span)].astype(jnp.float32)
+
         def flag_rows(b):
-            return jnp.broadcast_to(keep[s, b], (span, span)).T
+            return jnp.broadcast_to(keep_row(s, b), (span, span)).T
 
         def add_flux(x, u, v):
             w = x.astype(jnp.float32) * u + turn(x).astype(jnp.float32) * v
@@ -251,7 +269,7 @@
                 x = block(p)
                 c = block(q)
                 sx = scaled_of(x)
-                w = flag_rows(p) * keep[s, q]
+                w = flag_rows(p) * keep_row(s, q)
                 rre = (w * (work[s, u, 0].astype(jnp.float32) - tn(sx, c))).astype(jnp.bfloat16)
                 rim = (w * (work[s, u, 1].astype(jnp.float32) - tn(turn(sx), c))).astype(jnp.bfloat16)
                 work[s, u, 0] = rre
@@ -270,8 +288,8 @@
                 sb = scaled_of(c)
                 pre = jnp.where(hi, tn(sx, x), tn(c, sb))
                 pim = jnp.where(hi, tn(turn(sx), x), tn(c, turn(sb)))
-                w = jnp.where(hi, flag_rows(p) * keep[s, p], 0.0) + jnp.where(
-                    lo, flag_rows(q) * keep[s, q], 0.0)
+                w = jnp.where(hi, flag_rows(p) * keep_row(s, p), 0.0) + jnp.where(
+                    lo, flag_rows(q) * keep_row(s, q), 0.0)
                 rre = (w * (work[s, u, 0].astype(jnp.float32) - pre)).astype(jnp.bfloat16)
                 rim = (w * (work[s, u, 1].astype(jnp.float32) - pim)).astype(jnp.bfloat16)
                 work[s, u, 0] = rre
@@ -303,11 +321,18 @@
     def tidy(s):
         for u in range(units):
             res_copy(s, u).wait()
+        def z_sent(zi, yi):
+            src = own.at[s]
+            pl.when(jnp.logical_and(zi <= z, z < Z - 1))(lambda: up(src, s, zi, yi).wait_send())
+            pl.when(jnp.logical_and(zi >= z, z > 0))(lambda: down(src, s, zi, yi).wait_send())
+
         for zi in range(Z):
-            pl.when(jnp.logical_and(zi <= z, z < Z - 1))(lambda: up(own.at[s], s, zi).wait_send())
-            pl.when(jnp.logical_and(zi >= z, z > 0))(lambda: down(own.at[s], s, zi).wait_send())
+            z_sent(zi, y)
+            if early:
+                pl.when(s < early)(lambda: z_sent(zi, yother))
             if Y > 1:
-                across(own.at[s], s, zi).wait_send()
+                pl.when(jnp.logical_or(s >= early, zi == z))(
+                    lambda: across(own.at[s], s, zi).wait_send())
             for yi in range(Y):
                 mate(own.at[s], s, zi, yi).wait_send()
     each(tidy, slots)
@@ -330,12 +355,8 @@
     units, slots, _, span, _ = visibility.shape
     per_group = station_beam.shape[2]
     antennas = station_beam.shape[3]
-    keep_all = 1.0 - antenna_flags.astype(jnp.float32)
-    keep_all = keep_all.reshape(slots, BLOCKS, 1, span)
-    own, brightness = build_factors(
-        station_beam, antenna_uvw, source_dirs, source_flux, visible_list
-    )
-    bright = jnp.pad(brightness.T, ((0, 0), (0, 128 - slots)))
+    listed = jnp.pad(visible_list.astype(jnp.float32).T, ((0, 0), (0, 128 - slots)))
+    pool_flux = source_flux.astype(jnp.float32)[None]
     dims = (Z, Y, slots, units, per_group, span, -1.0 / (8.0 * antennas))
     vmem = pl.BlockSpec(memory_space=pltpu.VMEM)
     hbm = pl.BlockSpec(memory_space=pl.ANY)
@@ -347,17 +368,20 @@
             jax.ShapeDtypeStruct(visibility.shape, jnp.bfloat16),
             jax.ShapeDtypeStruct((per_group, 128), jnp.float32),
         ),
-        in_specs=[vmem, vmem, vmem, hbm],
+        in_specs=[vmem] * 6 + [hbm],
         out_specs=(hbm, vmem),
         scratch_shapes=[
+            pltpu.VMEM((slots, BLOCKS, 2 * per_group, span), jnp.bfloat16),
+            pltpu.VMEM((per_group, 128), jnp.float32),
+            pltpu.VMEM((per_group, 128), jnp.bfloat16),
             pltpu.VMEM((slots, BLOCKS, T, 2 * per_group, span), jnp.bfloat16),
             pltpu.VMEM((T, per_group, 128), jnp.bfloat16),
             pltpu.VMEM((slots, units, 2, span, span), jnp.bfloat16),
             pltpu.VMEM((T, per_group, 128), jnp.float32),
             pltpu.VMEM((T, per_group, 128), jnp.float32),
             dma((slots, T)),
-            dma((slots, Z)),
-            dma((slots, Z)),
+            dma((slots, Z * Y)),
+            dma((slots, Z * Y)),
             dma((slots, Z)),
             dma((slots, Z * Y)),
             dma((slots,)),
@@ -371,7 +395,7 @@
         compiler_params=pltpu.CompilerParams(
             collective_id=0, has_side_effects=True, vmem_limit_bytes=64 * 1024 * 1024 - 2 * 65536
         ),
-    )(own, bright, keep_all, visibility)
+    )(station_beam, antenna_uvw, source_dirs, pool_flux, listed, antenna_flags, visibility)
     return residual, flux[:, :slots].T
 
 

time: 242 us -> 221 us (0.913)
  other arithmetic: 15 us -> 1.91 us
  Pallas kernels: 216 us -> 209 us
    another operation x2 -> x0, other arithmetic: 10.5 us -> none
    pallas_call x1, Pallas kernels: 216 us -> 209 us  [per_device(): pl.pallas_call(functools.partial(kernel, dims), name='predict_pull', out_...]
    unnamed x4 -> x3, local copies, waits for them, and re-layouts: 5.9 us -> 7.07 us
where the time goes in v2:
time: 221 us; the launch traced here: 220 us
  Pallas kernels  209 us (95%)
  local copies, waits for them, and re-layouts  8.47 us (4%)
    pallas_call x1, Pallas kernels, per_device(): pl.pallas_call(functools.partial(kernel, dims), name='predict_pull', out_...  209 us
    unnamed x3, local copies, waits for them, and re-layouts  7.07 us

profile of v2, /device:TPU:0, one launch (start us, length us, event | category | flops | bytes accessed | tf_op | source)
XLA Modules:
  0.0 220.4 jit_solution(6436927363999250027)
XLA Ops:
  0.6 1.2 broadcast_in_dim.7
  1.8 0.7 convert_element_type.6
  2.5 0.1 copy.12
  2.6 0.6 pad.4.listed
  3.2 1.8 copy.13.uvw
  5.0 209.3 %predict_pull.1 = (bf16[2,8,2,256,256]{4,3,2,1,0:T(8,128)(2,1)}, f32[32,128]{1,0:T(8,128)}) custom-call(bf16[8,2,32,2048]{3,2,1,0:T(8,128)(2,1)} %beam.1, f32[8,3,2048]{2,1,0:T(4,128)} %copy.13.uvw, f32[2,256]{1,0:T(2,128)} %dirs.1, f32[1,256]{1,0:T(1,128)} %bitcast.5, f32[32,128]{1,0:T(8,128)} %pad.4.listed, s32[8,2048]{1,0:T(8,128)} %flags.1, ...), custom_call_target="tpu_custom_call" | custom-call | tf_op jit(solution)/shard_map/predict_pull/pallas_call | solution.py:364
  214.3 0.7 slice_bitcast_fusion
  215.1 0.7 copy.14
  215.7 4.6 %copy.16 = bf16[2,8,2,256,256]{4,3,2,1,0:T(8,128)(2,1)} copy(bf16[2,8,2,256,256]{4,3,2,1,0:T(8,128)(2,1)} %get-tuple-element.12) | data formatting | bytes 8388608

commit v3 on v2

--- a/solution.py
+++ b/solution.py
@@ -62,6 +62,7 @@
 
     other = dev(z, y, 1 - core)
     early = slots // 8 if Y > 1 else 0
+    late_from = slots - early
     yother = (y + 1) % Y
 
     def rc(src, s, sh, target, sem):
@@ -183,7 +184,7 @@
         arrived(s, sh)
         onward(s, zi, y, upward, not upward)
         if Y > 1:
-            pl.when(s >= early)(lambda: across(gath.at[s, :, sh], s, zi).start())
+            pl.when(s < late_from)(lambda: across(gath.at[s, :, sh], s, zi).start())
         mate(gath.at[s, :, sh], s, zi, y).start()
 
     def z_step(d, s):
@@ -194,7 +195,7 @@
         sh = dev(zi, yother, core)
         arrived(s, sh)
         if early:
-            pl.when(s < early)(lambda: onward(s, zi, yother, upward, downward))
+            pl.when(s >= late_from)(lambda: onward(s, zi, yother, upward, downward))
         mate(gath.at[s, :, sh], s, zi, yother).start()
 
     def y_step(d, s):
@@ -329,9 +330,9 @@
         for zi in range(Z):
             z_sent(zi, y)
             if early:
-                pl.when(s < early)(lambda: z_sent(zi, yother))
+                pl.when(s >= late_from)(lambda: z_sent(zi, yother))
             if Y > 1:
-                pl.when(jnp.logical_or(s >= early, zi == z))(
+                pl.when(jnp.logical_or(s < late_from, zi == z))(
                     lambda: across(own.at[s], s, zi).wait_send())
             for yi in range(Y):
                 mate(own.at[s], s, zi, yi).wait_send()

time: 221 us -> 215 us (0.973)
  Pallas kernels: 209 us -> 204 us
    pallas_call x1, Pallas kernels: 209 us -> 204 us  [per_device(): pl.pallas_call(functools.partial(kernel, dims), name='predict_pull', out_...]
where the time goes in v3:
time: 215 us
  Pallas kernels  204 us (95%)
  local copies, waits for them, and re-layouts  8.47 us (4%)
    pallas_call x1, Pallas kernels, per_device(): pl.pallas_call(functools.partial(kernel, dims), name='predict_pull', out_...  204 us
    unnamed x3, local copies, waits for them, and re-layouts  7.07 us

profile of v3, /device:TPU:0, one launch (start us, length us, event | category | flops | bytes accessed | tf_op | source)
XLA Modules:
  0.0 215.1 jit_solution(16476416369709291259)
XLA Ops:
  0.6 1.2 broadcast_in_dim.7
  1.8 0.7 convert_element_type.6
  2.5 0.1 copy.12
  2.6 0.6 pad.4.listed
  3.2 1.8 copy.13.uvw
  5.0 204.1 %predict_pull.1 = (bf16[2,8,2,256,256]{4,3,2,1,0:T(8,128)(2,1)}, f32[32,128]{1,0:T(8,128)}) custom-call(bf16[8,2,32,2048]{3,2,1,0:T(8,128)(2,1)} %beam.1, f32[8,3,2048]{2,1,0:T(4,128)} %copy.13.uvw, f32[2,256]{1,0:T(2,128)} %dirs.1, f32[1,256]{1,0:T(1,128)} %bitcast.5, f32[32,128]{1,0:T(8,128)} %pad.4.listed, s32[8,2048]{1,0:T(8,128)} %flags.1, ...), custom_call_target="tpu_custom_call" | custom-call | tf_op jit(solution)/shard_map/predict_pull/pallas_call | solution.py:365
  209.1 0.7 slice_bitcast_fusion
  209.8 0.7 copy.14
  210.5 4.6 %copy.16 = bf16[2,8,2,256,256]{4,3,2,1,0:T(8,128)(2,1)} copy(bf16[2,8,2,256,256]{4,3,2,1,0:T(8,128)(2,1)} %get-tuple-element.12) | data formatting | bytes 8388608

commit v4 on v3

--- a/solution.py
+++ b/solution.py
@@ -211,7 +211,7 @@
         z_step(d, s)
         y_step(d - 1, s)
 
-    for d in range(1, Z):
+    for d in range(1, Z - 1):
         each(functools.partial(hop_step, d), slots)
 
     def bright_wait(k):
@@ -311,7 +311,12 @@
             arrived(s, 2 * i + 1 - core)
         compute(s)
 
-    each(last_step, slots)
+    def far_step(s):
+        if Z > 1:
+            pl.when(s < slots)(lambda: hop_step(Z - 1, s))
+        pl.when(s > 0)(lambda: last_step(s - 1))
+
+    each(far_step, slots + 1)
 
     def flux_step(k):
         target = (me + k + 1) % T

time: 215 us -> 209 us (0.972)
  Pallas kernels: 204 us -> 198 us
    pallas_call x1, Pallas kernels: 204 us -> 198 us  [per_device(): pl.pallas_call(functools.partial(kernel, dims), name='predict_pull', out_...]
where the time goes in v4:
time: 209 us
  Pallas kernels  198 us (95%)
  local copies, waits for them, and re-layouts  8.47 us (4%)
    pallas_call x1, Pallas kernels, per_device(): pl.pallas_call(functools.partial(kernel, dims), name='predict_pull', out_...  198 us
    unnamed x3, local copies, waits for them, and re-layouts  7.07 us

profile of v4, /device:TPU:0, one launch (start us, length us, event | category | flops | bytes accessed | tf_op | source)
XLA Modules:
  0.0 208.7 jit_solution(15833939821913613531)
XLA Ops:
  0.6 1.2 broadcast_in_dim.7
  1.8 0.7 convert_element_type.6
  2.5 0.1 copy.12
  2.6 0.6 pad.4.listed
  3.2 1.8 copy.13.uvw
  5.0 197.6 %predict_pull.1 = (bf16[2,8,2,256,256]{4,3,2,1,0:T(8,128)(2,1)}, f32[32,128]{1,0:T(8,128)}) custom-call(bf16[8,2,32,2048]{3,2,1,0:T(8,128)(2,1)} %beam.1, f32[8,3,2048]{2,1,0:T(4,128)} %copy.13.uvw, f32[2,256]{1,0:T(2,128)} %dirs.1, f32[1,256]{1,0:T(1,128)} %bitcast.5, f32[32,128]{1,0:T(8,128)} %pad.4.listed, s32[8,2048]{1,0:T(8,128)} %flags.1, ...), custom_call_target="tpu_custom_call" | custom-call | tf_op jit(solution)/shard_map/predict_pull/pallas_call | solution.py:370
  202.6 0.7 slice_bitcast_fusion
  203.4 0.7 copy.14
  204.0 4.6 %copy.16 = bf16[2,8,2,256,256]{4,3,2,1,0:T(8,128)(2,1)} copy(bf16[2,8,2,256,256]{4,3,2,1,0:T(8,128)(2,1)} %get-tuple-element.12) | data formatting | bytes 8388608
